TPU v7x, 32 devices: a whole 2x2x4 slice. The times are simulated.
32 devices in a mesh: dp: 4 (over y, x), mx: 4 (over z), my: 2 (over core).
Axes of the slice: x: 2, y: 2, z: 4, core: 2. Of those that a mesh axis runs over, the one named last changes fastest.
Arguments:
- tokens: bfloat16 [8192, 2048], P(('dp', 'my'), 'mx'), may hold values from -6 to 6
- output_grad: bfloat16 [8192, 2048], P(('dp', 'my'), 'mx'), may hold values from -6 to 6
- picture_starts: int32 [8, 2], P('dp'), may hold values from 0 to 768, as said below
- norm1_gain: float32 [2048], P('mx'), may hold values from 0.5 to 1.5
- query_weight: bfloat16 [2048, 2048], P('mx', 'my'), may hold values from -0.5 to 0.5
- key_weight: bfloat16 [2048, 512], P('mx', 'my'), may hold values from -0.5 to 0.5
- value_weight: bfloat16 [2048, 512], P('mx', 'my'), may hold values from -0.125 to 0.125
- out_weight: bfloat16 [2048, 2048], P('my', 'mx'), may hold values from -2 to 2
- norm2_gain: float32 [2048], P('mx'), may hold values from 0.5 to 1.5
- gate_weight: bfloat16 [2048, 8192], P('mx', 'my'), may hold values from -0.125 to 0.125
- up_weight: bfloat16 [2048, 8192], P('mx', 'my'), may hold values from -0.125 to 0.125
- down_weight: bfloat16 [8192, 2048], P('my', 'mx'), may hold values from -0.5 to 0.5
Outputs:
- output: bfloat16 [8192, 2048], P(('dp', 'my'), 'mx')
- input_grad: bfloat16 [8192, 2048], P(('dp', 'my'), 'mx')
- grad_norm1: float32 [2048], P('mx')
- grad_query: float32 [2048, 2048], P('mx', 'my')
- grad_key: float32 [2048, 512], P('mx', 'my')
- grad_value: float32 [2048, 512], P('mx', 'my')
- grad_out: float32 [2048, 2048], P('my', 'mx')
- grad_norm2: float32 [2048], P('mx')
- grad_gate: float32 [2048, 8192], P('mx', 'my')
- grad_up: float32 [2048, 8192], P('mx', 'my')
- grad_down: float32 [8192, 2048], P('my', 'mx')
Inputs may be any that keep to these rules, and one draw needn't show every extreme that they name: `picture_starts`: piece p of a sequence starts at a position from p * 512 to (p + 1) * 512 - 256, so the pieces of a sequence never intersect and lie inside it; some sequence has its first piece at position 0 and some sequence has its last piece ending at the sequence's end.
All inputs are finite; a program needn't handle non-finite values.
Results may differ from a plain program's by a relative error of at most 0.02.
Values may be sent and summed in bfloat16 or wider, within the bound.
No kernel may reach another device: no remote copies, remote signals or barrier semaphores. Data moves between devices by JAX's collectives and lax.ppermute only.
A program may use at most 384 MiB of HBM per device.

v0:
```python
import jax
import jax.numpy as jnp
from jax import lax
from jax.sharding import PartitionSpec as P

D = 2048
HEAD = 64
LEN = 1024
PIECE = 256


epsilon = 1e-05
rope_base = 10000000.0
branch_scale = 0.22
score_scale = 0.015625
masked_score = -1e30


def rope_tables(positions, head_width):
    half_width = head_width // 2
    steps_idx = jnp.arange(half_width, dtype=jnp.float32)
    freqs = jnp.exp(-jnp.log(jnp.float32(rope_base)) * 2.0 * steps_idx / head_width)
    angles = positions.astype(jnp.float32)[:, None] * freqs[None, :]
    cosine = jnp.cos(angles)
    sine = jnp.sin(angles)
    return (jnp.concatenate([cosine, cosine], 1), jnp.concatenate([sine, sine], 1))


def rotate_half(values):
    half_width = values.shape[-1] // 2
    return jnp.concatenate([-values[..., half_width:], values[..., :half_width]], -1)


def apply_rope(values, cosine, sine):
    return values * cosine[:, None, :] + rotate_half(values) * sine[:, None, :]


def rope_back(values, cosine, sine):
    return values * cosine[:, None, :] - rotate_half(values) * sine[:, None, :]


def row_info(row_ids, starts, seq_length, piece_length):
    sequence_ids = row_ids // seq_length
    position = row_ids % seq_length
    choose_row = (
        sequence_ids[:, None] == jnp.arange(starts.shape[0], dtype=jnp.int32)[None, :]
    ).astype(jnp.int32)
    piece_begin = jnp.sum(choose_row[:, :, None] * starts[None, :, :], axis=1)
    inside = (position[:, None] >= piece_begin) & (position[:, None] < piece_begin + piece_length)
    number = jnp.arange(1, starts.shape[1] + 1, dtype=jnp.int32)
    piece_id = jnp.sum(inside.astype(jnp.int32) * number[None, :], axis=1) - 1
    return (sequence_ids, position, piece_id)


def allowed(query_facts, key_facts):
    query_seq, query_pos, query_piece = query_facts
    key_seq, key_pos, key_piece = key_facts
    same_sequence = query_seq[:, None] == key_seq[None, :]
    before = key_pos[None, :] <= query_pos[:, None]
    piece_both = (query_piece[:, None] >= 0) & (query_piece[:, None] == key_piece[None, :])
    return same_sequence & (before | piece_both)


def product(left, weight, flipped):
    if flipped:
        return lax.dot_general(
            left, weight, (((1,), (1,)), ((), ())), preferred_element_type=jnp.float32
        )
    return jnp.dot(left, weight, preferred_element_type=jnp.float32)


def outer_sum(left, right):
    return lax.dot_general(
        left, right, (((0,), (0,)), ((), ())), preferred_element_type=jnp.float32
    )


def feature_sum(values):
    return lax.psum(jnp.sum(values, axis=1), "mx")


def norm_forward(stream, gain, full_width):
    inverse = lax.rsqrt(feature_sum(stream * stream)[:, None] / full_width + epsilon)
    return (inverse, (stream * inverse * gain[None, :]).astype(jnp.bfloat16))


def norm_backward(stream, inverse, gain, grad_normed, full_width):
    scaled = gain[None, :] * grad_normed
    row_total = feature_sum(stream * scaled)[:, None]
    grad_stream = inverse * scaled - stream * inverse * inverse * inverse * row_total / full_width
    grad_gain = jnp.sum(grad_normed * stream * inverse, axis=0)
    return (grad_stream, grad_gain)


def stream_gather(values):
    return lax.all_gather(values, "my", axis=0, tiled=True)


def block_gather(values):
    return lax.all_gather(values, "mx", axis=0, tiled=True)


def width_sum(gathered, weight):
    return lax.psum_scatter(product(gathered, weight, True), "mx", scatter_dimension=0, tiled=True)


def head_sum(gathered, weight, flipped):
    return lax.psum_scatter(
        product(gathered, weight, flipped), "my", scatter_dimension=0, tiled=True
    )


def widen_rows(gathered):
    return lax.all_to_all(gathered, "mx", split_axis=0, concat_axis=1, tiled=True)


def fold_rows(wide_rows, weight):
    return jnp.dot(
        wide_rows,
        lax.all_gather(weight, "mx", axis=0, tiled=True),
        preferred_element_type=jnp.float32,
    )


def fold_columns(wide_rows, weight):
    return lax.dot_general(
        wide_rows,
        lax.all_gather(weight, "mx", axis=1, tiled=True),
        (((1,), (1,)), ((), ())),
        preferred_element_type=jnp.float32,
    )


def head_scores(query, key_head, allowed_pairs):
    scores = (
        jnp.einsum("qgd,kd->qgk", query, key_head, preferred_element_type=jnp.float32) * score_scale
    )
    return jnp.where(allowed_pairs[:, None, :], scores, masked_score)


def head_forward(query, key_head, value_head, allowed_pairs):
    scores = head_scores(query, key_head, allowed_pairs)
    row_max = jnp.max(scores, axis=-1, keepdims=True)
    shifted = jnp.exp(scores - row_max)
    row_total = jnp.sum(shifted, axis=-1, keepdims=True)
    probs = shifted / row_total
    mixed = jnp.einsum(
        "qgk,kd->qgd", probs.astype(jnp.bfloat16), value_head, preferred_element_type=jnp.float32
    )
    return (mixed, (row_max + jnp.log(row_total))[..., 0])


def head_backward(query, key_head, value_head, grad_out, log_total, allowed_pairs):
    scores = head_scores(query, key_head, allowed_pairs)
    probs = jnp.exp(scores - log_total[..., None])
    grad_probs = jnp.einsum("qgd,kd->qgk", grad_out, value_head, preferred_element_type=jnp.float32)
    row_dot = jnp.sum(probs * grad_probs, axis=-1, keepdims=True)
    grad_scores = (probs * (grad_probs - row_dot)).astype(jnp.bfloat16)
    grad_query = (
        jnp.einsum("qgk,kd->qgd", grad_scores, key_head, preferred_element_type=jnp.float32)
        * score_scale
    )
    grad_key = (
        jnp.einsum("qgk,qgd->kd", grad_scores, query, preferred_element_type=jnp.float32)
        * score_scale
    )
    grad_value = jnp.einsum(
        "qgk,qgd->kd", probs.astype(jnp.bfloat16), grad_out, preferred_element_type=jnp.float32
    )
    return (grad_query, grad_key, grad_value)


def shards(
    tokens,
    output_grad,
    picture_starts,
    norm1_gain,
    query_weight,
    key_weight,
    value_weight,
    out_weight,
    norm2_gain,
    gate_weight,
    up_weight,
    down_weight,
):
    mx_count = lax.axis_size("mx")
    my_count = lax.axis_size("my")
    local_rows = tokens.shape[0]
    group_rows = local_rows * my_count
    attn_rows = group_rows // mx_count
    query_cols = query_weight.shape[1]
    key_cols = key_weight.shape[1]
    query_heads = query_cols // HEAD
    key_heads = key_cols // HEAD
    kv_group = query_heads // key_heads
    hidden_cols = gate_weight.shape[1]
    attn_in = jnp.concatenate([query_weight, key_weight, value_weight], axis=1)
    ffn_in = jnp.concatenate([gate_weight, up_weight], axis=1)
    stream = tokens.astype(jnp.float32)
    inverse_one, normed_one = norm_forward(stream, norm1_gain, D)
    normed_one_all = stream_gather(normed_one)
    projected = fold_rows(widen_rows(normed_one_all), attn_in)
    query_ids = lax.axis_index("mx") * attn_rows + jnp.arange(attn_rows, dtype=jnp.int32)
    cosine, sine = rope_tables(query_ids % LEN, HEAD)
    query_rot = apply_rope(
        projected[:, :query_cols].reshape(attn_rows, query_heads, HEAD), cosine, sine
    )
    query_rot = query_rot.astype(jnp.bfloat16)
    key_rot = apply_rope(
        projected[:, query_cols : query_cols + key_cols].reshape(attn_rows, key_heads, HEAD),
        cosine,
        sine,
    )
    key_local = jnp.concatenate(
        [key_rot.reshape(attn_rows, key_cols), projected[:, query_cols + key_cols :]], axis=1
    ).astype(jnp.bfloat16)
    key_all = lax.all_gather(key_local, "mx", axis=0, tiled=True)
    key_ids = jnp.arange(group_rows, dtype=jnp.int32)
    allowed_pairs = allowed(
        row_info(query_ids, picture_starts, LEN, PIECE),
        row_info(key_ids, picture_starts, LEN, PIECE),
    )
    query_split = query_rot.reshape(attn_rows, key_heads, kv_group, HEAD).transpose(1, 0, 2, 3)
    key_split = key_all[:, :key_cols].reshape(group_rows, key_heads, HEAD).transpose(1, 0, 2)
    value_split = key_all[:, key_cols:].reshape(group_rows, key_heads, HEAD).transpose(1, 0, 2)
    mixed, log_totals = lax.map(
        lambda head_parts: head_forward(head_parts[0], head_parts[1], head_parts[2], allowed_pairs),
        (query_split, key_split, value_split),
    )
    attn_out = mixed.transpose(1, 0, 2, 3).reshape(attn_rows, query_cols).astype(jnp.bfloat16)
    attn_all = block_gather(attn_out)
    hidden_one = stream + branch_scale * head_sum(attn_all, out_weight, False)
    inverse_two, normed_two = norm_forward(hidden_one, norm2_gain, D)
    normed_two_all = stream_gather(normed_two)
    gate_up = fold_rows(widen_rows(normed_two_all), ffn_in)
    gate_val = gate_up[:, :hidden_cols]
    up_val = gate_up[:, hidden_cols:]
    sigma = jax.nn.sigmoid(gate_val)
    silu_gate = gate_val * sigma
    hidden_units = (silu_gate * up_val).astype(jnp.bfloat16)
    hidden_all = block_gather(hidden_units)
    hidden_two = hidden_one + branch_scale * head_sum(hidden_all, down_weight, False)
    output = hidden_two.astype(jnp.bfloat16)
    grad_two = output_grad.astype(jnp.float32)
    branch_two = (branch_scale * grad_two).astype(jnp.bfloat16)
    branch_two_all = stream_gather(branch_two)
    grad_down = outer_sum(hidden_all, branch_two_all)
    grad_hidden = fold_columns(widen_rows(branch_two_all), down_weight)
    grad_gate_val = (grad_hidden * up_val * sigma * (1.0 + gate_val * (1.0 - sigma))).astype(
        jnp.bfloat16
    )
    grad_up_val = (grad_hidden * silu_gate).astype(jnp.bfloat16)
    grad_gate_up = jnp.concatenate([grad_gate_val, grad_up_val], axis=1)
    grad_gate_up_all = block_gather(grad_gate_up)
    grad_ffn_in = outer_sum(normed_two_all, grad_gate_up_all)
    grad_gate = grad_ffn_in[:, :hidden_cols]
    grad_up = grad_ffn_in[:, hidden_cols:]
    grad_normed_two = head_sum(grad_gate_up_all, ffn_in, True)
    grad_stream_two, grad_norm2 = norm_backward(
        hidden_one, inverse_two, norm2_gain, grad_normed_two, D
    )
    grad_one = grad_two + grad_stream_two
    branch_one = (branch_scale * grad_one).astype(jnp.bfloat16)
    branch_one_all = stream_gather(branch_one)
    grad_out = outer_sum(attn_all, branch_one_all)
    grad_attn = width_sum(branch_one_all, out_weight).astype(jnp.bfloat16)
    grad_attn_split = grad_attn.reshape(attn_rows, key_heads, kv_group, HEAD).transpose(1, 0, 2, 3)
    grad_q, grad_k, grad_v = lax.map(
        lambda head_parts: head_backward(
            head_parts[0], head_parts[1], head_parts[2], head_parts[3], head_parts[4], allowed_pairs
        ),
        (query_split, key_split, value_split, grad_attn_split, log_totals),
    )
    key_terms = jnp.concatenate(
        [
            grad_k.transpose(1, 0, 2).reshape(group_rows, key_cols),
            grad_v.transpose(1, 0, 2).reshape(group_rows, key_cols),
        ],
        axis=1,
    )
    key_owned = lax.psum_scatter(
        key_terms.astype(jnp.bfloat16), "mx", scatter_dimension=0, tiled=True
    ).astype(jnp.float32)
    grad_q_pre = rope_back(
        grad_q.transpose(1, 0, 2, 3).reshape(attn_rows, query_heads, HEAD), cosine, sine
    )
    grad_k_pre = rope_back(
        key_owned[:, :key_cols].reshape(attn_rows, key_heads, HEAD), cosine, sine
    )
    grad_projected = jnp.concatenate(
        [
            grad_q_pre.reshape(attn_rows, query_cols),
            grad_k_pre.reshape(attn_rows, key_cols),
            key_owned[:, key_cols:],
        ],
        axis=1,
    ).astype(jnp.bfloat16)
    grad_projected_all = block_gather(grad_projected)
    grad_attn_in = outer_sum(normed_one_all, grad_projected_all)
    grad_query = grad_attn_in[:, :query_cols]
    grad_key = grad_attn_in[:, query_cols : query_cols + key_cols]
    grad_value = grad_attn_in[:, query_cols + key_cols :]
    grad_normed_one = head_sum(grad_projected_all, attn_in, True)
    grad_stream_one, grad_norm1 = norm_backward(stream, inverse_one, norm1_gain, grad_normed_one, D)
    input_grad = (grad_one + grad_stream_one).astype(jnp.bfloat16)
    grad_query, grad_key, grad_value, grad_out, grad_gate, grad_up, grad_down = (
        lax.psum(grad_query.astype(jnp.bfloat16), "dp").astype(jnp.float32),
        lax.psum(grad_key.astype(jnp.bfloat16), "dp").astype(jnp.float32),
        lax.psum(grad_value.astype(jnp.bfloat16), "dp").astype(jnp.float32),
        lax.psum(grad_out.astype(jnp.bfloat16), "dp").astype(jnp.float32),
        lax.psum(grad_gate.astype(jnp.bfloat16), "dp").astype(jnp.float32),
        lax.psum(grad_up.astype(jnp.bfloat16), "dp").astype(jnp.float32),
        lax.psum(grad_down.astype(jnp.bfloat16), "dp").astype(jnp.float32),
    )
    grad_norm1, grad_norm2 = lax.psum((grad_norm1, grad_norm2), ("dp", "my"))
    return (
        output,
        input_grad,
        grad_norm1,
        grad_query,
        grad_key,
        grad_value,
        grad_out,
        grad_norm2,
        grad_gate,
        grad_up,
        grad_down,
    )


def solution(mesh):
    placed = (
        P(("dp", "my"), "mx"),
        P(("dp", "my"), "mx"),
        P("dp", None),
        P("mx"),
        P("mx", "my"),
        P("mx", "my"),
        P("mx", "my"),
        P("my", "mx"),
        P("mx"),
        P("mx", "my"),
        P("mx", "my"),
        P("my", "mx"),
    )
    return jax.shard_map(
        shards,
        mesh=mesh,
        in_specs=placed,
        out_specs=(
            P(("dp", "my"), "mx"),
            P(("dp", "my"), "mx"),
            P("mx"),
            P("mx", "my"),
            P("mx", "my"),
            P("mx", "my"),
            P("my", "mx"),
            P("mx"),
            P("mx", "my"),
            P("mx", "my"),
            P("my", "mx"),
        ),
        check_vma=False,
    )
```

profile of v0, /device:TPU:0, one launch (start us, length us, event | category | flops | bytes accessed | tf_op | source)
XLA Modules:
  0.0 3158.8 jit_solution(17961203384813808073)
XLA Ops:
  8.9 13.5 psum.91
  44.1 104.5 %all-to-all-done = bf16[4,512,512]{1,2,0:T(8,128)(2,1)} async-done(((bf16[4,512,512]{1,2,0:T(8,128)(2,1)}), bf16[4,512,512]{1,2,0:T(8,128)(2,1)}, u32[]{:S(2)}, u32[]{:S(2)}) %all-to-all-start) | async-done | bytes 2097184 | tf_op jit(solution)/shard_map/all_to_all | solution.py:114
  148.5 45.2 %all-gather.15.cloned.1.call-done = bf16[2048,1536]{1,0:T(8,128)(2,1)} async-done(((bf16[512,1536]{1,0:T(8,128)(2,1)}), bf16[2048,1536]{1,0:T(8,128)(2,1)}) %all-gather.15.cloned.1.call-update) | async-done | bytes 6291472 | tf_op jit(solution)/shard_map/all_gather | solution.py:120
  218.7 30.5 all-gather.17.cloned.1.call-done
  254.8 69.0 %while.30 = (s32[]{:T(128)}, bf16[4,512,4,64]{1,3,2,0:T(8,128)(2,1)S(1)}, f32[4,512,4]{1,2,0:T(4,128)}, bf16[4,512,4,64]{1,3,2,0:T(8,128)(2,1)}, bf16[4,2048,64]...) while((s32[]{:T(128)}, ...), condition=%wide.region_9.10_spmd.clone.clone, body=%wide.region_6.9_spmd.clone.sunk.clone | while | flops 1130362880 | bytes 55936124 | solution.py:227
  324.9 79.7 %all-gather.19.cloned.1.call-done = bf16[2048,1024]{0,1:T(8,128)(2,1)} async-done(((bf16[512,1024]{0,1:T(8,128)(2,1)}), bf16[2048,1024]{0,1:T(8,128)(2,1)}) %all-gather.19.cloned.1.call-update) | async-done | bytes 4194320 | tf_op jit(solution)/shard_map/all_gather | solution.py:100
  411.2 10.6 reduce-scatter.7.cloned.1.call-done
  424.1 12.1 psum.92
  464.4 73.6 %all-to-all-done.1 = bf16[4,512,512]{1,2,0:T(8,128)(2,1)} async-done(((bf16[4,512,512]{1,2,0:T(8,128)(2,1)}), bf16[4,512,512]{1,2,0:T(8,128)(2,1)}, u32[]{:S(2)}, u32[]{:S(2)}) %all-to-all-start.1) | async-done | bytes 2097184 | tf_op jit(solution)/shard_map/all_to_all | solution.py:114
  537.9 21.0 all-to-all-start.2
  559.0 530.0 %all-gather.23.cloned.1.call-done = bf16[2048,8192]{1,0:T(8,128)(2,1)} async-done(((bf16[512,8192]{1,0:T(8,128)(2,1)}), bf16[2048,8192]{1,0:T(8,128)(2,1)}) %all-gather.23.cloned.1.call-update) | async-done | bytes 33554448 | tf_op jit(solution)/shard_map/all_gather | solution.py:120
  1089.0 27.6 fusion.97
  1116.6 259.8 %all-gather.29.cloned.1.call-done = bf16[4096,2048]{1,0:T(8,128)(2,1)} async-done(((bf16[4096,512]{1,0:T(8,128)(2,1)}), bf16[4096,2048]{1,0:T(8,128)(2,1)}) %all-gather.29.cloned.1.call-update) | async-done | bytes 16777232 | tf_op jit(solution)/shard_map/all_gather | solution.py:128
  1376.5 22.1 multiply_convert_fusion.2
  1407.3 559.0 %all-gather.31.cloned.1.call-done = bf16[2048,8192]{1,0:T(8,128)(2,1)} async-done(((bf16[512,8192]{1,0:T(8,128)(2,1)}), bf16[2048,8192]{1,0:T(8,128)(2,1)}) %all-gather.31.cloned.1.call-update) | async-done | bytes 33554448 | tf_op jit(solution)/shard_map/all_gather | solution.py:100
  1966.2 25.0 fusion.99
  1991.3 261.5 %all-gather.25.cloned.1.call-done = bf16[2048,4096]{1,0:T(8,128)(2,1)} async-done(((bf16[512,4096]{1,0:T(8,128)(2,1)}), bf16[2048,4096]{1,0:T(8,128)(2,1)}) %all-gather.25.cloned.1.call-update) | async-done | bytes 16777232 | tf_op jit(solution)/shard_map/all_gather | solution.py:100
  2252.8 14.9 fusion.98
  2270.4 10.0 psum.93
  2286.5 12.0 all-gather.33.cloned.1.call-done
  2305.9 145.9 %reduce-scatter.13.cloned.1.call-done = f32[512,1024]{1,0:T(8,128)} async-done(((f32[2048,1024]{1,0:T(8,128)}), f32[512,1024]{1,0:T(8,128)}) %reduce-scatter.13.cloned.1.call-update) | async-done | bytes 2097168 | tf_op jit(solution)/shard_map/reduce_scatter | solution.py:104
  2454.9 161.2 %while.31 = (s32[]{:T(128)}, f32[4,512,4,64]{1,3,2,0:T(8,128)}, bf16[4,2048,64]{1,2,0:T(8,128)(2,1)}, bf16[4,2048,64]{1,2,0:T(8,128)(2,1)}, bf16[4,512,4,64]{1,3...) while((s32[]{:T(128)}, f32[4,512,4,64]{1,3,2,0:T(8,128)}, ...), condition=%wide.region_20.21_spmd.clone.clone, body=%wide.region_18.20_spmd.clone.sunk.clone | while | flops 2753820672 | bytes 141913808 | solution.py:269
  2462.0 10.6 multiply_reduce_fusion.8
  2502.2 10.6 multiply_reduce_fusion.8
  2542.3 10.6 multiply_reduce_fusion.8
  2582.5 10.6 multiply_reduce_fusion.8
  2621.1 42.6 %reduce-scatter.15.cloned.1.call-done = bf16[512,512]{0,1:T(8,128)(2,1)} async-done(((bf16[2048,512]{0,1:T(8,128)(2,1)}), bf16[512,512]{0,1:T(8,128)(2,1)}) %reduce-scatter.15.cloned.1.call-update) | async-done | bytes 524304 | tf_op jit(solution)/shard_map/reduce_scatter | solution.py:282
  2667.4 114.6 %all-gather.35.cloned.1.call-done = bf16[2048,1536]{0,1:T(8,128)(2,1)} async-done(((bf16[512,1536]{0,1:T(8,128)(2,1)}), bf16[2048,1536]{0,1:T(8,128)(2,1)}) %all-gather.35.cloned.1.call-update) | async-done | bytes 6291472 | tf_op jit(solution)/shard_map/all_gather | solution.py:100
  2790.1 14.6 convolution_convert_fusion.1
  2804.7 26.0 convolution_convert_fusion
  2854.3 15.2 all-reduce
  2882.0 249.2 %all-reduce.4.cloned.1.call-done = (bf16[512,1024]{1,0:T(8,128)(2,1)}, bf16[512,256]{1,0:T(8,128)(2,1)}, bf16[512,256]{1,0:T(8,128)(2,1)}, bf16[1024,512]{1,0:T(...) async-done(((bf16[512,1024]{1,0:T(8,128)(2,1)}, bf16[512,256]{1,0:T(8,128)(2,1)}, bf16[512,256]{1,0:T(8,128)(2,1)}, ...) | async-done | bytes 15204368 | tf_op jit(solution)/shard_map/psum | solution.py:308
  (265 shorter events, 379.8 us)
Async XLA Ops:
  7.2 397.4 %copy-start = (bf16[1024,512]{1,0:T(8,128)(2,1)S(1)}, bf16[1024,512]{1,0:T(8,128)(2,1)}, u32[]{:S(2)}) copy-start(bf16[1024,512]{1,0:T(8,128)(2,1)} %param.23) | copy-start | bytes 3145732
  7.2 19.6 copy-start.26
  7.2 19.7 copy-start.27
  7.2 27.2 all-gather.13.cloned.1.call-start
  25.5 168.3 %all-gather.15.cloned.1.call-start = ((), (), s32[]{:S(2)}) async-start(), calls=%async_computation.10 | async-start | bytes 7864320 | tf_op jit(solution)/shard_map/all_gather | solution.py:120
  38.6 110.0 %all-to-all-start = ((bf16[4,512,512]{1,2,0:T(8,128)(2,1)}), bf16[4,512,512]{1,2,0:T(8,128)(2,1)}, u32[]{:S(2)}, u32[]{:S(2)}) async-start(bf16[4,512,512]{1,2,0:T(8,128)(2,1)} %copy.46), calls=%async_computation | async-start | bytes 4194304 | tf_op jit(solution)/shard_map/all_to_all | solution.py:114
  43.4 205.8 %all-gather.17.cloned.1.call-start = ((), (), s32[]{:S(2)}) async-start(), calls=%async_computation.11 | async-start | bytes 2621440 | tf_op jit(solution)/shard_map/all_gather | solution.py:218
  43.8 173.3 %copy-start.14 = (f32[512,64]{0,1:T(8,128)}, f32[512,64]{0,1:T(8,128)S(1)}, u32[]{:S(2)}) copy-start(f32[512,64]{0,1:T(8,128)S(1)} %get-tuple-element.288) | copy-start | bytes 393220
  43.8 173.3 %copy-start.16 = (f32[512,64]{0,1:T(8,128)}, f32[512,64]{0,1:T(8,128)S(1)}, u32[]{:S(2)}) copy-start(f32[512,64]{0,1:T(8,128)S(1)} %get-tuple-element.287) | copy-start | bytes 393220
  204.3 200.3 %all-gather.19.cloned.1.call-start = ((), (), s32[]{:S(2)}) async-start(), calls=%async_computation.12 | async-start | bytes 5242880 | tf_op jit(solution)/shard_map/all_gather | solution.py:100
  218.7 36.1 %copy-start.11 = (bf16[4,512,4,64]{1,3,2,0:T(8,128)(2,1)S(1)}, bf16[4,512,4,64]{1,3,2,0:T(8,128)(2,1)}, u32[]{:S(2)}) copy-start(bf16[4,512,4,64]{1,3,2,0:T(8,128)(2,1)} %broadcast_convert_fusion) | copy-start | bytes 3145732
  323.9 87.3 %copy-start.5 = (bf16[4,2048,64]{1,2,0:T(8,128)(2,1)}, bf16[4,2048,64]{1,2,0:T(8,128)(2,1)S(1)}, u32[]{:S(2)}) copy-start(bf16[4,2048,64]{1,2,0:T(8,128)(2,1)S(1)} %get-tuple-element.677) | copy-start | bytes 3145732
  324.9 97.0 %reduce-scatter.7.cloned.1.call-start = ((), (), s32[]{:S(2)}) async-start(), calls=%async_computation.13 | async-start | bytes 6291456 | tf_op jit(solution)/shard_map/reduce_scatter | solution.py:108
  411.2 25.1 copy-start.31
  411.2 37.5 %all-gather.21.cloned.1.call-start = ((), (), s32[]{:S(2)}) async-start(), calls=%async_computation.14 | async-start | bytes 3145728 | tf_op jit(solution)/shard_map/all_gather | solution.py:96
  437.5 22.8 all-gather.27.cloned.1.call-start
  439.9 649.1 %all-gather.23.cloned.1.call-start = ((), (), s32[]{:S(2)}) async-start(), calls=%async_computation.15 | async-start | bytes 41943040 | tf_op jit(solution)/shard_map/all_gather | solution.py:120
  447.9 928.5 %all-gather.29.cloned.1.call-start = ((), (), s32[]{:S(2)}) async-start(), calls=%async_computation.19 | async-start | bytes 20971520 | tf_op jit(solution)/shard_map/all_gather | solution.py:128
  452.8 85.1 %all-to-all-start.1 = ((bf16[4,512,512]{1,2,0:T(8,128)(2,1)}), bf16[4,512,512]{1,2,0:T(8,128)(2,1)}, u32[]{:S(2)}, u32[]{:S(2)}) async-start(bf16[4,512,512]{1,2,0:T(8,128)(2,1)} %copy.54), calls=%async_computation.2 | async-start | bytes 4194304 | tf_op jit(solution)/shard_map/all_to_all | solution.py:114
  537.9 578.7 %all-to-all-start.2 = ((bf16[4,512,512]{1,2,0:T(8,128)(2,1)}), bf16[4,512,512]{1,2,0:T(8,128)(2,1)}, u32[]{:S(2)}, u32[]{:S(2)}) async-start(bf16[4,512,512]{1,2,0:T(8,128)(2,1)} %copy.55), calls=%async_computation.4 | async-start | bytes 4194304 | tf_op jit(solution)/shard_map/all_to_all | solution.py:114
  559.0 1407.2 %all-gather.31.cloned.1.call-start = ((), (), s32[]{:S(2)}) async-start(), calls=%async_computation.20 | async-start | bytes 41943040 | tf_op jit(solution)/shard_map/all_gather | solution.py:100
  1406.5 846.3 %all-gather.25.cloned.1.call-start = ((), (), s32[]{:S(2)}) async-start(), calls=%async_computation.16 | async-start | bytes 20971520 | tf_op jit(solution)/shard_map/all_gather | solution.py:100
  1407.2 860.5 %reduce-scatter.11.cloned.1.call-start = ((), (), s32[]{:S(2)}) async-start(), calls=%async_computation.21 | async-start | bytes 6291456 | tf_op jit(solution)/shard_map/reduce_scatter | solution.py:108
  1991.3 290.7 %reduce-scatter.9.cloned.1.call-start = ((), (), s32[]{:S(2)}) async-start(), calls=%async_computation.17 | async-start | bytes 6291456 | tf_op jit(solution)/shard_map/reduce_scatter | solution.py:108
  2267.7 30.8 all-gather.33.cloned.1.call-start
  2286.4 165.4 %reduce-scatter.13.cloned.1.call-start = ((), (), s32[]{:S(2)}) async-start(), calls=%async_computation.23 | async-start | bytes 10485760 | tf_op jit(solution)/shard_map/reduce_scatter | solution.py:104
  2305.8 357.9 %reduce-scatter.15.cloned.1.call-start = ((), (), s32[]{:S(2)}) async-start(), calls=%async_computation.24 | async-start | bytes 2621440 | tf_op jit(solution)/shard_map/reduce_scatter | solution.py:282
  2619.3 162.7 %all-gather.35.cloned.1.call-start = ((), (), s32[]{:S(2)}) async-start(), calls=%async_computation.25 | async-start | bytes 7864320 | tf_op jit(solution)/shard_map/all_gather | solution.py:100
  2664.8 117.2 %copy-start.7 = (bf16[512,1536]{1,0:T(8,128)(2,1)S(1)}, bf16[512,1536]{1,0:T(8,128)(2,1)}, u32[]{:S(2)}) copy-start(bf16[512,1536]{1,0:T(8,128)(2,1)} %copy-done.6) | copy-start | bytes 4718596
  2667.3 183.2 %reduce-scatter.17.cloned.1.call-start = ((), (), s32[]{:S(2)}) async-start(), calls=%async_computation.26 | async-start | bytes 6291456 | tf_op jit(solution)/shard_map/reduce_scatter | solution.py:108
  2790.0 341.2 %all-reduce.4.cloned.1.call-start = ((), (), s32[]{:S(2)}) async-start(), calls=%async_computation.27 | async-start | bytes 30408704 | tf_op jit(solution)/shard_map/psum | solution.py:308
  2851.7 26.6 copy-start.3
  (32 other events, 121.3 us)
Sparse Core Ops, SparseCore 0:
  25.6 8.7 all-gather.12
  36.0 157.7 all-gather.14
  204.4 44.7 all-gather.16
  325.0 79.5 all-gather.18
  411.3 10.5 reduce-scatter.6
  437.6 8.7 all-gather.20
  448.5 11.7 all-gather.26
  462.4 626.5 all-gather.22
  1090.6 285.8 all-gather.28
  1406.6 559.5 all-gather.30
  1967.8 284.9 all-gather.24
  2255.5 10.2 reduce-scatter.10
  2268.6 13.3 reduce-scatter.8
  2286.5 11.8 all-gather.32
  2306.0 145.7 reduce-scatter.12
  2619.4 44.2 reduce-scatter.14
  2667.5 114.4 all-gather.34
  2790.1 10.2 reduce-scatter.16
  2850.6 280.5 all-reduce.3
where the time goes:
time: 3160 us
  waiting for transfers between devices  2530 us (80%)
  matrix products  316 us (10%)
  other arithmetic  148 us (5%)
  blocking collectives  59.6 us (2%)
  local copies, waits for them, and re-layouts  57.1 us (2%)
  starting transfers between devices  31.7 us (1%)
    all_gather x4, waiting for transfers between devices, block_gather(): return lax.all_gather(values, 'mx', axis=0, tiled=True)  1010 us
    all_gather x2, waiting for transfers between devices, fold_rows(): lax.all_gather(weight, 'mx', axis=0, tiled=True)  575 us
    all_gather x1, waiting for transfers between devices, fold_columns(): lax.all_gather(weight, 'mx', axis=1, tiled=True)  260 us
    psum x1, waiting for transfers between devices, shards(): lax.psum(grad_query.astype(jnp.bfloat16), 'dp').astype(jnp.float32)  249 us
    all_to_all x3, waiting for transfers between devices, widen_rows(): lax.all_to_all(gathered, 'mx', split_axis=0, concat_axis=1, tiled=True)  178 us
    reduce_scatter x1, waiting for transfers between devices, width_sum(): lax.psum_scatter(product(gathered, weight, True), 'mx', scatter_dimension...  146 us
  transfers between devices with their start and end apart: 22, of which 18 were waited for; matrix products, arithmetic and copies ran while one was open for 6% of the time, Pallas kernels for 0%

commit v1 on v0

v1 whole, which is shorter than its diff:
```python
import jax
import jax.numpy as jnp
from jax import lax
from jax.sharding import PartitionSpec as P

D = 2048
HEAD = 64
LEN = 1024
PIECE = 256


epsilon = 1e-05
rope_base = 10000000.0
branch_scale = 0.22
score_scale = 0.015625
masked_score = -1e30


def rope_tables(positions, head_width):
    half_width = head_width // 2
    steps_idx = jnp.arange(half_width, dtype=jnp.float32)
    freqs = jnp.exp(-jnp.log(jnp.float32(rope_base)) * 2.0 * steps_idx / head_width)
    angles = positions.astype(jnp.float32)[:, None] * freqs[None, :]
    cosine = jnp.cos(angles)
    sine = jnp.sin(angles)
    return (jnp.concatenate([cosine, cosine], 1), jnp.concatenate([sine, sine], 1))


def rotate_half(values):
    half_width = values.shape[-1] // 2
    return jnp.concatenate([-values[..., half_width:], values[..., :half_width]], -1)


def apply_rope(values, cosine, sine):
    return values * cosine + rotate_half(values) * sine


def rope_back(values, cosine, sine):
    return values * cosine - rotate_half(values) * sine


def product(left, weight, flipped):
    if flipped:
        return lax.dot_general(
            left, weight, (((1,), (1,)), ((), ())), preferred_element_type=jnp.float32
        )
    return jnp.dot(left, weight, preferred_element_type=jnp.float32)


def outer_sum(left, right):
    return lax.dot_general(
        left, right, (((0,), (0,)), ((), ())), preferred_element_type=jnp.float32
    )


def head_scores(query, key_head, allowed_pairs):
    scores = (
        jnp.einsum("qgd,kd->qgk", query, key_head, preferred_element_type=jnp.float32) * score_scale
    )
    return jnp.where(allowed_pairs[:, None, :], scores, masked_score)


def head_forward(query, key_head, value_head, allowed_pairs):
    scores = head_scores(query, key_head, allowed_pairs)
    row_max = jnp.max(scores, axis=-1, keepdims=True)
    shifted = jnp.exp(scores - row_max)
    row_total = jnp.sum(shifted, axis=-1, keepdims=True)
    probs = shifted / row_total
    mixed = jnp.einsum(
        "qgk,kd->qgd", probs.astype(jnp.bfloat16), value_head, preferred_element_type=jnp.float32
    )
    return (mixed, (row_max + jnp.log(row_total))[..., 0])


def head_backward(query, key_head, value_head, grad_out, log_total, allowed_pairs):
    scores = head_scores(query, key_head, allowed_pairs)
    probs = jnp.exp(scores - log_total[..., None])
    grad_probs = jnp.einsum("qgd,kd->qgk", grad_out, value_head, preferred_element_type=jnp.float32)
    row_dot = jnp.sum(probs * grad_probs, axis=-1, keepdims=True)
    grad_scores = (probs * (grad_probs - row_dot)).astype(jnp.bfloat16)
    grad_query = (
        jnp.einsum("qgk,kd->qgd", grad_scores, key_head, preferred_element_type=jnp.float32)
        * score_scale
    )
    grad_key = (
        jnp.einsum("qgk,qgd->kd", grad_scores, query, preferred_element_type=jnp.float32)
        * score_scale
    )
    grad_value = jnp.einsum(
        "qgk,qgd->kd", probs.astype(jnp.bfloat16), grad_out, preferred_element_type=jnp.float32
    )
    return (grad_query, grad_key, grad_value)


PLANE = ("dp", "my")


def plane_gather(values):
    return lax.all_gather(values, PLANE, axis=0, tiled=True)


def plane_scatter(values):
    return lax.psum_scatter(
        values.astype(jnp.bfloat16), PLANE, scatter_dimension=0, tiled=True
    ).astype(jnp.float32)


def to_rows(values):
    return lax.all_to_all(values, "mx", split_axis=0, concat_axis=1, tiled=True)


def to_tiles(values):
    return lax.all_to_all(values, "mx", split_axis=1, concat_axis=0, tiled=True)


def line_gather(values, axis):
    return lax.all_gather(values, "mx", axis=axis, tiled=True)


def line_scatter(values, axis):
    return lax.psum_scatter(
        values.astype(jnp.bfloat16), "mx", scatter_dimension=axis, tiled=True
    )


def norm_forward(stream, gain):
    mean = jnp.mean(stream * stream, axis=1, keepdims=True)
    inverse = lax.rsqrt(mean + epsilon)
    return (inverse, (stream * inverse * gain[None, :]).astype(jnp.bfloat16))


def norm_backward(stream, inverse, gain, grad_normed):
    scaled = gain[None, :] * grad_normed
    row_mean = jnp.mean(stream * scaled, axis=1, keepdims=True)
    grad_stream = inverse * scaled - stream * inverse * inverse * inverse * row_mean
    grad_gain = jnp.sum(grad_normed * stream * inverse, axis=0)
    return (grad_stream, grad_gain)


def piece_of(position, begins):
    inside = (position >= begins) & (position < begins + PIECE)
    number = jnp.arange(1, begins.shape[-1] + 1, dtype=jnp.int32)
    return jnp.sum(jnp.where(inside, number, 0), axis=-1)


def shards(
    tokens,
    output_grad,
    picture_starts,
    norm1_gain,
    query_weight,
    key_weight,
    value_weight,
    out_weight,
    norm2_gain,
    gate_weight,
    up_weight,
    down_weight,
):
    mx_count = lax.axis_size("mx")
    dp_count = lax.axis_size("dp")
    dp_index = lax.axis_index("dp")
    mx_index = lax.axis_index("mx")
    chunk = LEN // mx_count
    seqs = dp_count * lax.axis_size("my")
    rows = seqs * chunk
    query_cols = query_weight.shape[1] // dp_count
    query_heads = query_cols // HEAD
    key_heads = key_weight.shape[1] // HEAD
    share = max(1, dp_count // key_heads)
    key_cols = key_weight.shape[1] * share // dp_count
    own_keys = key_cols // HEAD
    kv_group = query_heads // own_keys
    hidden = gate_weight.shape[1] // dp_count

    def cols(weight, width, index):
        return lax.dynamic_slice_in_dim(weight, index * width, width, axis=1)

    def rows_of(weight, width):
        return lax.dynamic_slice_in_dim(weight, dp_index * width, width, axis=0)

    key_index = dp_index // share
    attn_in = line_gather(
        jnp.concatenate(
            [
                cols(query_weight, query_cols, dp_index),
                cols(key_weight, key_cols, key_index),
                cols(value_weight, key_cols, key_index),
            ],
            axis=1,
        ),
        0,
    )
    attn_back = line_gather(rows_of(out_weight, query_cols), 1)
    ffn_in = line_gather(
        jnp.concatenate(
            [cols(gate_weight, hidden, dp_index), cols(up_weight, hidden, dp_index)], axis=1
        ),
        0,
    )
    ffn_back = line_gather(rows_of(down_weight, hidden), 1)
    gains = line_gather(jnp.stack([norm1_gain, norm2_gain]), 1)
    gain_one, gain_two = gains[0], gains[1]
    starts = lax.all_gather(picture_starts, "dp", axis=0, tiled=True)

    stream = to_rows(tokens).astype(jnp.float32)
    grad_two = to_rows(output_grad).astype(jnp.float32)
    inverse_one, normed_one = norm_forward(stream, gain_one)
    normed_one_all = plane_gather(normed_one)
    projected = product(normed_one_all, attn_in, False)

    query_pos = mx_index * chunk + jnp.arange(chunk, dtype=jnp.int32)
    key_pos = jnp.arange(LEN, dtype=jnp.int32)
    cosine, sine = rope_tables(query_pos, HEAD)
    cosine = cosine[None, :, None, :]
    sine = sine[None, :, None, :]
    query_piece = piece_of(query_pos[None, :, None], starts[:, None, :])
    key_piece = piece_of(key_pos[None, :, None], starts[:, None, :])
    before = key_pos[None, None, :] <= query_pos[None, :, None]
    same = (query_piece[:, :, None] > 0) & (query_piece[:, :, None] == key_piece[:, None, :])
    allowed_pairs = before | same

    query_rot = apply_rope(
        projected[:, :query_cols].reshape(seqs, chunk, query_heads, HEAD), cosine, sine
    ).astype(jnp.bfloat16)
    key_rot = apply_rope(
        projected[:, query_cols : query_cols + key_cols].reshape(seqs, chunk, own_keys, HEAD),
        cosine,
        sine,
    ).astype(jnp.bfloat16)
    value_own = projected[:, query_cols + key_cols :].astype(jnp.bfloat16)
    key_local = jnp.concatenate(
        [key_rot.reshape(seqs, chunk, key_cols), value_own.reshape(seqs, chunk, key_cols)], axis=2
    )
    key_all = line_gather(key_local, 1)

    query_split = query_rot.reshape(seqs, chunk, own_keys, kv_group, HEAD)
    query_split = query_split.transpose(0, 2, 1, 3, 4).reshape(-1, chunk, kv_group, HEAD)

    def split_keys(values):
        values = values.reshape(seqs, LEN, own_keys, HEAD)
        return values.transpose(0, 2, 1, 3).reshape(-1, LEN, HEAD)

    key_split = split_keys(key_all[:, :, :key_cols])
    value_split = split_keys(key_all[:, :, key_cols:])
    pairs = jnp.repeat(allowed_pairs, own_keys, axis=0)
    mixed, log_totals = lax.map(
        lambda p: head_forward(p[0], p[1], p[2], p[3]),
        (query_split, key_split, value_split, pairs),
    )

    def join_heads(values):
        values = values.reshape(seqs, own_keys, chunk, kv_group, HEAD).transpose(0, 2, 1, 3, 4)
        return values.reshape(rows, query_cols)

    def split_heads(values):
        values = values.reshape(seqs, chunk, own_keys, kv_group, HEAD).transpose(0, 2, 1, 3, 4)
        return values.reshape(-1, chunk, kv_group, HEAD)

    attn_out = join_heads(mixed).astype(jnp.bfloat16)
    hidden_one = stream + branch_scale * plane_scatter(product(attn_out, attn_back, False))
    inverse_two, normed_two = norm_forward(hidden_one, gain_two)
    normed_two_all = plane_gather(normed_two)
    gate_up = product(normed_two_all, ffn_in, False)
    gate_val = gate_up[:, :hidden]
    up_val = gate_up[:, hidden:]
    sigma = jax.nn.sigmoid(gate_val)
    silu_gate = gate_val * sigma
    hidden_units = (silu_gate * up_val).astype(jnp.bfloat16)
    hidden_two = hidden_one + branch_scale * plane_scatter(product(hidden_units, ffn_back, False))
    output = to_tiles(hidden_two.astype(jnp.bfloat16))

    branch_two = (branch_scale * grad_two).astype(jnp.bfloat16)
    branch_two_all = plane_gather(branch_two)
    grad_down = outer_sum(hidden_units, branch_two_all)
    grad_hidden = product(branch_two_all, ffn_back, True)
    grad_gate_val = (grad_hidden * up_val * sigma * (1.0 + gate_val * (1.0 - sigma))).astype(
        jnp.bfloat16
    )
    grad_up_val = (grad_hidden * silu_gate).astype(jnp.bfloat16)
    grad_gate_up = jnp.concatenate([grad_gate_val, grad_up_val], axis=1)
    grad_ffn_in = outer_sum(normed_two_all, grad_gate_up)
    grad_normed_two = plane_scatter(product(grad_gate_up, ffn_in, True))
    grad_stream_two, grad_norm2 = norm_backward(hidden_one, inverse_two, gain_two, grad_normed_two)
    grad_one = grad_two + grad_stream_two
    branch_one_all = plane_gather((branch_scale * grad_one).astype(jnp.bfloat16))
    grad_out = outer_sum(attn_out, branch_one_all)
    grad_attn = split_heads(product(branch_one_all, attn_back, True).astype(jnp.bfloat16))
    grad_q, grad_k, grad_v = lax.map(
        lambda p: head_backward(p[0], p[1], p[2], p[3], p[4], p[5]),
        (query_split, key_split, value_split, grad_attn, log_totals, pairs),
    )

    def join_keys(values):
        values = values.reshape(seqs, own_keys, LEN, HEAD).transpose(0, 2, 1, 3)
        return values.reshape(seqs, LEN, key_cols)

    key_terms = jnp.concatenate([join_keys(grad_k), join_keys(grad_v)], axis=2)
    key_owned = line_scatter(key_terms, 1).astype(jnp.float32)
    grad_q_pre = rope_back(
        join_heads(grad_q).reshape(seqs, chunk, query_heads, HEAD), cosine, sine
    )
    grad_k_pre = rope_back(
        key_owned[:, :, :key_cols].reshape(seqs, chunk, own_keys, HEAD), cosine, sine
    )
    grad_projected = jnp.concatenate(
        [
            grad_q_pre.reshape(rows, query_cols),
            grad_k_pre.reshape(rows, key_cols),
            key_owned[:, :, key_cols:].reshape(rows, key_cols),
        ],
        axis=1,
    ).astype(jnp.bfloat16)
    grad_attn_in = outer_sum(normed_one_all, grad_projected)
    grad_normed_one = plane_scatter(product(grad_projected, attn_in, True))
    grad_stream_one, grad_norm1 = norm_backward(stream, inverse_one, gain_one, grad_normed_one)
    input_grad = to_tiles((grad_one + grad_stream_one).astype(jnp.bfloat16))

    def spread_cols(own):
        return lax.all_gather(own, "dp", axis=1, tiled=True).astype(jnp.float32)

    def spread_rows(own):
        return lax.all_gather(own, "dp", axis=0, tiled=True).astype(jnp.float32)

    def spread_keys(own):
        every = lax.all_gather(own, "dp", axis=0).astype(jnp.float32)
        every = every.reshape(dp_count // share, share, -1, key_cols).sum(axis=1)
        return every.transpose(1, 0, 2).reshape(every.shape[1], -1)

    grad_down = spread_rows(line_scatter(grad_down, 1))
    own_ffn = line_scatter(grad_ffn_in, 0)
    grad_gate = spread_cols(own_ffn[:, :hidden])
    grad_up = spread_cols(own_ffn[:, hidden:])
    grad_out = spread_rows(line_scatter(grad_out, 1))
    own_attn = line_scatter(grad_attn_in, 0)
    grad_query = spread_cols(own_attn[:, :query_cols])
    grad_key = spread_keys(own_attn[:, query_cols : query_cols + key_cols])
    grad_value = spread_keys(own_attn[:, query_cols + key_cols :])
    norms = lax.psum(jnp.stack([grad_norm1, grad_norm2]), ("dp", "mx", "my"))
    norms = lax.dynamic_slice_in_dim(norms, mx_index * norm1_gain.shape[0], norm1_gain.shape[0], 1)
    return (
        output,
        input_grad,
        norms[0],
        grad_query,
        grad_key,
        grad_value,
        grad_out,
        norms[1],
        grad_gate,
        grad_up,
        grad_down,
    )


def solution(mesh):
    placed = (
        P(("dp", "my"), "mx"),
        P(("dp", "my"), "mx"),
        P("dp", None),
        P("mx"),
        P("mx", "my"),
        P("mx", "my"),
        P("mx", "my"),
        P("my", "mx"),
        P("mx"),
        P("mx", "my"),
        P("mx", "my"),
        P("my", "mx"),
    )
    return jax.shard_map(
        shards,
        mesh=mesh,
        in_specs=placed,
        out_specs=(
            P(("dp", "my"), "mx"),
            P(("dp", "my"), "mx"),
            P("mx"),
            P("mx", "my"),
            P("mx", "my"),
            P("mx", "my"),
            P("my", "mx"),
            P("mx"),
            P("mx", "my"),
            P("mx", "my"),
            P("my", "mx"),
        ),
        check_vma=False,
    )
```

time: 3160 us -> 1770 us (0.56)
  waiting for transfers between devices: 2530 us -> 1120 us
  blocking collectives: 59.6 us -> 175 us
  other arithmetic: 148 us -> 82.7 us
    all_gather x12 -> x14, waiting for transfers between devices: 1900 us -> 577 us  [the longest x4 220 us: plane_gather(): return lax.all_gather(values, PLANE, axis=0, tiled=True)]
    reduce_scatter x6 -> x9, waiting for transfers between devices: 201 us -> 543 us  [the longest x4 286 us: plane_scatter(): lax.psum_scatter(values.astype(jnp.bfloat16), PLANE, scatter_dimension=0,...]
    psum x1 -> x0, waiting for transfers between devices: 249 us -> none  [shards(): lax.psum(grad_query.astype(jnp.bfloat16), 'dp').astype(jnp.float32)]
    all_to_all x3, waiting for transfers between devices: 178 us -> 1.46 us  [the longest x2 1.45 us: to_tiles(): return lax.all_to_all(values, 'mx', split_axis=1, concat_axis=0, tiled=True)]
    all_gather x0 -> x4, blocking collectives: none -> 77.9 us  [the longest x1 45.3 us: line_gather(): return lax.all_gather(values, 'mx', axis=axis, tiled=True)]
    all_to_all x0 -> x1, blocking collectives: none -> 57.9 us  [to_rows(): return lax.all_to_all(values, 'mx', split_axis=0, concat_axis=1, tiled=True)]
    dot_general x3 -> x0, matrix products: 56 us -> none  [the longest x2 33.9 us: fold_rows(): jnp.dot(wide_rows, lax.all_gather(weight, 'mx', axis=0, tiled=True), pref...]
  transfers between devices with their start and end apart: 22 -> 26, of which waited for: 18 -> 20; matrix products, arithmetic and copies ran while one was open for 6% -> 13% of each run, Pallas kernels for 0% -> 0%
where the time goes in v1:
time: 1770 us; the launch traced here: 1760 us
  waiting for transfers between devices  1120 us (63%)
  matrix products  297 us (17%)
  blocking collectives  175 us (10%)
  other arithmetic  82.7 us (5%)
  local copies, waits for them, and re-layouts  54.2 us (3%)
  starting transfers between devices  18.3 us (1%)
    reduce_scatter x4, waiting for transfers between devices, plane_scatter(): lax.psum_scatter(values.astype(jnp.bfloat16), PLANE, scatter_dimension=0,...  286 us
    reduce_scatter x5, waiting for transfers between devices, line_scatter(): lax.psum_scatter(values.astype(jnp.bfloat16), 'mx', scatter_dimension=axi...  257 us
    all_gather x4, waiting for transfers between devices, plane_gather(): return lax.all_gather(values, PLANE, axis=0, tiled=True)  220 us
    all_gather x5, waiting for transfers between devices, line_gather(): return lax.all_gather(values, 'mx', axis=axis, tiled=True)  191 us
    all_gather x3, waiting for transfers between devices, spread_cols(): return lax.all_gather(own, 'dp', axis=1, tiled=True).astype(jnp.float32)  96.4 us
    all_gather x2, waiting for transfers between devices, spread_rows(): return lax.all_gather(own, 'dp', axis=0, tiled=True).astype(jnp.float32)  69.4 us
    dot_general x4, matrix products, product(): lax.dot_general(left, weight, (((1,), (1,)), ((), ())), preferred_element...  59.1 us
    all_to_all x1, blocking collectives, to_rows(): return lax.all_to_all(values, 'mx', split_axis=0, concat_axis=1, tiled=True)  57.9 us
  transfers between devices with their start and end apart: 26, of which 20 were waited for; matrix products, arithmetic and copies ran while one was open for 13% of the time, Pallas kernels for 0%

profile of v1, /device:TPU:0, one launch (start us, length us, event | category | flops | bytes accessed | tf_op | source)
XLA Modules:
  0.0 1764.2 jit_solution(13706677136220090018)
XLA Ops:
  15.8 45.3 %all_gather.61 = f32[2,2048]{1,0:T(2,128)S(1)} all-gather(f32[2,512]{1,0:T(2,128)S(1)} %pad_maximum_fusion.10), channel_id=1, replica_groups=mesh['dp'=4,'mx'=4,'my'=2] {'mx'}, dimensions={1}, use_global_device_ids=true | all-gather | bytes 20480 | tf_op jit(solution)/shard_map/all_gather | solution.py:117
  65.7 55.6 %all-gather.18.cloned.1.call-done = bf16[2048,2048]{1,0:T(8,128)(2,1)} async-done(((bf16[256,2048]{1,0:T(8,128)(2,1)}), bf16[2048,2048]{1,0:T(8,128)(2,1)}) %all-gather.18.cloned.1.call-update) | async-done | bytes 8388624 | tf_op jit(solution)/shard_map/all_gather | solution.py:99
  148.5 28.1 %all-gather.22.cloned.1.call-done = bf16[8,1024,128]{1,2,0:T(8,128)(2,1)} async-done(((bf16[8,256,128]{1,2,0:T(8,128)(2,1)}), bf16[8,1024,128]{1,2,0:T(8,128)(2,1)}) %all-gather.22.cloned.1.call-update) | async-done | bytes 2097168 | tf_op jit(solution)/shard_map/all_gather | solution.py:117
  179.7 57.7 %while.28 = (s32[]{:T(128)}, bf16[8,256,4,64]{1,3,2,0:T(8,128)(2,1)}, f32[8,256,4]{1,2,0:T(4,128)S(1)}, pred[8,256,1024]{2,1,0:T(8,128)(4,1)}, bf16[8,256,4,64]{...) while((s32[]{:T(128)}, bf16[8,256,4,64]{1,3,2,0:T(8,128)(2,1)}, ...), condition=%wide.region_6.7_spmd.clone, body=%wide.region_3.6_spmd.sunk.clone | while | flops 281017344 | bytes 14583893 | solution.py:247
  250.4 66.5 %reduce-scatter.10.cloned.1.call-done = bf16[256,2048]{1,0:T(8,128)(2,1)} async-done(((bf16[2048,2048]{1,0:T(8,128)(2,1)}), bf16[256,2048]{1,0:T(8,128)(2,1)}) %reduce-scatter.10.cloned.1.call-update) | async-done | bytes 1048592 | tf_op jit(solution)/shard_map/reduce_scatter | solution.py:103
  322.5 57.9 %all_to_all.64 = bf16[4,256,512]{2,1,0:T(8,128)(2,1)S(1)} all-to-all(bf16[4,256,512]{2,1,0:T(8,128)(2,1)} %bitcast.282), channel_id=1, replica_groups=mesh['dp'=4,'mx'=4,'my'=2] {'mx'}, dimensions={0} | all-to-all | bytes 2097152 | tf_op jit(solution)/shard_map/all_to_all | solution.py:109
  383.7 104.4 %all-gather.28.cloned.1.call-done = bf16[2048,2048]{1,0:T(8,128)(2,1)} async-done(((bf16[512,2048]{1,0:T(8,128)(2,1)}), bf16[2048,2048]{1,0:T(8,128)(2,1)}) %all-gather.28.cloned.1.call-update) | async-done | bytes 8388624 | tf_op jit(solution)/shard_map/all_gather | solution.py:117
  488.1 54.9 %all-gather.26.cloned.1.call-done = bf16[2048,2048]{1,0:T(8,128)(2,1)} async-done(((bf16[256,2048]{1,0:T(8,128)(2,1)}), bf16[2048,2048]{1,0:T(8,128)(2,1)}) %all-gather.26.cloned.1.call-update) | async-done | bytes 8388624 | tf_op jit(solution)/shard_map/all_gather | solution.py:99
  543.0 24.3 %fusion.93 = f32[2048,2048]{0,1:T(8,128)} fusion(bf16[2048,2048]{1,0:T(8,128)(2,1)} %all-gather.26.cloned.1.call-done, bf16[2048,2048]{1,0:T(8,128)(2,1)} %all-gather.28.cloned.1.call-done), kind=kOutput, calls=%fused_computation.183 | convolution fusion | flops 17179869184 | bytes 33554432 | tf_op jit(solution)/shard_map/dot_general | solution.py:47
  567.3 58.6 %all-gather.30.cloned.1.call-done = bf16[1024,2048]{1,0:T(8,128)(2,1)} async-done(((bf16[1024,512]{1,0:T(8,128)(2,1)}), bf16[1024,2048]{1,0:T(8,128)(2,1)}) %all-gather.30.cloned.1.call-update) | async-done | bytes 4194320 | tf_op jit(solution)/shard_map/all_gather | solution.py:117
  625.9 55.2 %all-gather.32.cloned.1.call-done = bf16[2048,2048]{1,0:T(8,128)(2,1)} async-done(((bf16[256,2048]{1,0:T(8,128)(2,1)}), bf16[2048,2048]{1,0:T(8,128)(2,1)}) %all-gather.32.cloned.1.call-update) | async-done | bytes 8388624 | tf_op jit(solution)/shard_map/all_gather | solution.py:99
  681.2 22.1 %multiply_convert_fusion.2 = (bf16[2048,1024]{0,1:T(8,128)(2,1)}, bf16[2048,1024]{0,1:T(8,128)(2,1)}, bf16[2048,1024]{0,1:T(8,128)(2,1)}) fusion(f32[2048,2048]{0,1:T(8,128)} %fusion.93, bf16[2048,2048]{1,0:T(8,128)(2,1)} %all-gather.32.cloned.1.call-done, bf16[1024,2048]{1,0:T(8,128)(2,1)} %all-gather.30.cloned.1.call-done), kind=kOutput, calls=%fused_computation.63 | convolution fusion | flops 8621391872 | bytes 41943040 | tf_op jit(solution)/shard_map/dot_general | solution.py:44
  703.3 24.1 %convolution_convert_fusion.2 = bf16[2048,2048]{1,0:T(8,128)(2,1)} fusion(bf16[2048,2048]{1,0:T(8,128)(2,1)} %all-gather.28.cloned.1.call-done, bf16[2048,1024]{0,1:T(8,128)(2,1)} %get-tuple-element.224, bf16[2048,1024]{0,1:T(8,128)(2,1)} %get-tuple-element.223), kind=kOutput, calls=%fused_computation.70 | convolution fusion | flops 17200840704 | bytes 25165824 | tf_op jit(solution)/shard_map/dot_general | solution.py:44
  727.5 71.6 %reduce-scatter.14.cloned.1.call-done = bf16[256,2048]{1,0:T(8,128)(2,1)} async-done(((bf16[2048,2048]{1,0:T(8,128)(2,1)}), bf16[256,2048]{1,0:T(8,128)(2,1)}) %reduce-scatter.14.cloned.1.call-update) | async-done | bytes 1048592 | tf_op jit(solution)/shard_map/reduce_scatter | solution.py:103
  803.9 54.3 %all-gather.34.cloned.1.call-done = bf16[2048,2048]{1,0:T(8,128)(2,1)} async-done(((bf16[256,2048]{1,0:T(8,128)(2,1)}), bf16[2048,2048]{1,0:T(8,128)(2,1)}) %all-gather.34.cloned.1.call-update) | async-done | bytes 8388624 | tf_op jit(solution)/shard_map/all_gather | solution.py:99
  867.5 109.9 %while.29 = (s32[]{:T(128)}, f32[8,256,4,64]{1,3,2,0:T(8,128)}, bf16[8,1024,64]{1,2,0:T(8,128)(2,1)}, bf16[8,1024,64]{1,2,0:T(8,128)(2,1)}, pred[8,256,1024]{2,1...) while((s32[]{:T(128)}, f32[8,256,4,64]{1,3,2,0:T(8,128)}, ...), condition=%wide.region_14.15_spmd.clone, body=%wide.region_12.14_spmd.sunk.clone | while | flops 686947328 | bytes 34505836 | solution.py:289
  980.5 13.8 convolution_convert_fusion.5
  994.4 23.9 %convolution_convert_fusion = bf16[2048,2048]{1,0:T(8,128)(2,1)} fusion(bf16[2048,2048]{1,0:T(8,128)(2,1)} %all-gather.26.cloned.1.call-done, bf16[2048,1024]{0,1:T(8,128)(2,1)} %get-tuple-element.224, bf16[2048,1024]{0,1:T(8,128)(2,1)} %get-tuple-element.223), kind=kOutput, calls=%fused_computation.68 | convolution fusion | flops 17200840704 | bytes 25165824 | tf_op jit(solution)/shard_map/dot_general | solution.py:51
  1040.9 14.3 convolution_convert_fusion.3
  1064.5 38.1 %reduce-scatter.26.cloned.1.call-done = bf16[1024,512]{1,0:T(8,128)(2,1)} async-done(((bf16[1024,2048]{1,0:T(8,128)(2,1)}), bf16[1024,512]{1,0:T(8,128)(2,1)}) %reduce-scatter.26.cloned.1.call-update) | async-done | bytes 1048592 | tf_op jit(solution)/shard_map/reduce_scatter | solution.py:121
  1102.6 147.9 %reduce-scatter.24.cloned.1.call-done = bf16[512,2048]{1,0:T(8,128)(2,1)} async-done(((bf16[2048,2048]{1,0:T(8,128)(2,1)}), bf16[512,2048]{1,0:T(8,128)(2,1)}) %reduce-scatter.24.cloned.1.call-update) | async-done | bytes 2097168 | tf_op jit(solution)/shard_map/reduce_scatter | solution.py:121
  1254.3 26.2 %reduce-scatter.22.cloned.1.call-done = bf16[256,512]{1,0:T(8,128)(2,1)} async-done(((bf16[256,2048]{1,0:T(8,128)(2,1)}), bf16[256,512]{1,0:T(8,128)(2,1)}) %reduce-scatter.22.cloned.1.call-update) | async-done | bytes 262160 | tf_op jit(solution)/shard_map/reduce_scatter | solution.py:121
  1280.6 73.9 %reduce-scatter.18.cloned.1.call-done = bf16[256,2048]{1,0:T(8,128)(2,1)} async-done(((bf16[2048,2048]{1,0:T(8,128)(2,1)}), bf16[256,2048]{1,0:T(8,128)(2,1)}) %reduce-scatter.18.cloned.1.call-update) | async-done | bytes 1048592 | tf_op jit(solution)/shard_map/reduce_scatter | solution.py:103
  1356.4 73.5 %reduce-scatter.12.cloned.1.call-done = bf16[256,2048]{1,0:T(8,128)(2,1)} async-done(((bf16[2048,2048]{1,0:T(8,128)(2,1)}), bf16[256,2048]{1,0:T(8,128)(2,1)}) %reduce-scatter.12.cloned.1.call-update) | async-done | bytes 1048592 | tf_op jit(solution)/shard_map/reduce_scatter | solution.py:103
  1440.1 44.9 %reduce-scatter.20.cloned.1.call-done = bf16[512,384]{1,0:T(8,128)(2,1)} async-done(((bf16[2048,384]{1,0:T(8,128)(2,1)}), bf16[512,384]{1,0:T(8,128)(2,1)}) %reduce-scatter.20.cloned.1.call-update) | async-done | bytes 393232 | tf_op jit(solution)/shard_map/reduce_scatter | solution.py:121
  1495.3 47.7 %all-gather.44.cloned.1.call-done = bf16[4096,512]{1,0:T(8,128)(2,1)} async-done(((bf16[1024,512]{1,0:T(8,128)(2,1)}), bf16[4096,512]{1,0:T(8,128)(2,1)}) %all-gather.44.cloned.1.call-update) | async-done | bytes 4194320 | tf_op jit(solution)/shard_map/all_gather | solution.py:323
  1549.7 48.1 %all-gather.40.cloned.1.call-done = bf16[512,4096]{1,0:T(8,128)(2,1)} async-done(((bf16[512,1024]{1,0:T(8,128)(2,1)}), bf16[512,4096]{1,0:T(8,128)(2,1)}) %all-gather.40.cloned.1.call-update) | async-done | bytes 4194320 | tf_op jit(solution)/shard_map/all_gather | solution.py:320
  1604.5 48.4 %all-gather.42.cloned.1.call-done = bf16[512,4096]{1,0:T(8,128)(2,1)} async-done(((bf16[512,1024]{1,0:T(8,128)(2,1)}), bf16[512,4096]{1,0:T(8,128)(2,1)}) %all-gather.42.cloned.1.call-update) | async-done | bytes 4194320 | tf_op jit(solution)/shard_map/all_gather | solution.py:320
  1659.5 21.7 %all-gather.38.cloned.1.call-done = bf16[1024,512]{1,0:T(8,128)(2,1)} async-done(((bf16[256,512]{1,0:T(8,128)(2,1)}), bf16[1024,512]{1,0:T(8,128)(2,1)}) %all-gather.38.cloned.1.call-update) | async-done | bytes 1048592 | tf_op jit(solution)/shard_map/all_gather | solution.py:323
  1684.2 12.1 all-gather
  1697.5 12.2 all-gather.1
  1715.6 38.9 %psum.7 = f32[2,2048]{1,0:T(2,128)S(1)} all-reduce(f32[2,2048]{1,0:T(2,128)S(1)} %pad_maximum_fusion.9), channel_id=1, replica_groups=mesh['dp'=4,'mx'=4,'my'=2] {'dp','mx','my'}, use_global_device_ids=true, to_apply=%region_20.21 | all-reduce | flops 4096 | bytes 32768 | tf_op jit(solution)/shard_map/psum | solution.py:339
  (334 shorter events, 340.1 us)
Async XLA Ops:
  7.2 54.0 %all-to-all-start = ((bf16[4,256,512]{2,1,0:T(8,128)(2,1)}), bf16[4,256,512]{2,1,0:T(8,128)(2,1)S(1)}, u32[]{:S(2)}, u32[]{:S(2)}) async-start(bf16[4,256,512]{2,1,0:T(8,128)(2,1)} %bitcast.281), calls=%async_computation | async-start | bytes 2097152 | tf_op jit(solution)/shard_map/all_to_all | solution.py:109
  13.7 52.0 %all-gather.20.cloned.1.call-start = ((), (), s32[]{:S(2)}) async-start(), calls=%async_computation.14 | async-start | bytes 1966080 | tf_op jit(solution)/shard_map/all_gather | solution.py:117
  15.8 105.5 %all-gather.18.cloned.1.call-start = ((), (), s32[]{:S(2)}) async-start(), calls=%async_computation.13 | async-start | bytes 9437184 | tf_op jit(solution)/shard_map/all_gather | solution.py:99
  61.2 740.6 %copy-start.21 = (f32[1,2048]{1,0:T(1,128)}, f32[1,2048]{1,0:T(1,128)S(1)}, u32[]{:S(2)}) copy-start(f32[1,2048]{1,0:T(1,128)S(1)} %get-tuple-element.247) | copy-start | bytes 24580
  63.7 738.1 %copy-start.2 = (f32[4,32,8,512]{3,2,0,1:T(8,128)}, f32[4,32,8,512]{3,2,0,1:T(8,128)S(1)}, u32[]{:S(2)}) copy-start(f32[4,32,8,512]{3,2,0,1:T(8,128)S(1)} %copy.125) | copy-start | bytes 6291460
  65.4 111.2 %all-gather.22.cloned.1.call-start = ((), (), s32[]{:S(2)}) async-start(), calls=%async_computation.15 | async-start | bytes 2621440 | tf_op jit(solution)/shard_map/all_gather | solution.py:117
  130.2 109.4 %all-gather.24.cloned.1.call-start = ((), (), s32[]{:S(2)}) async-start(), calls=%async_computation.16 | async-start | bytes 1310720 | tf_op jit(solution)/shard_map/all_gather | solution.py:117
  131.9 184.9 %reduce-scatter.10.cloned.1.call-start = ((), (), s32[]{:S(2)}) async-start(), calls=%async_computation.17 | async-start | bytes 9437184 | tf_op jit(solution)/shard_map/reduce_scatter | solution.py:103
  247.0 241.1 %all-gather.28.cloned.1.call-start = ((), (), s32[]{:S(2)}) async-start(), calls=%async_computation.19 | async-start | bytes 10485760 | tf_op jit(solution)/shard_map/all_gather | solution.py:117
  250.3 292.7 %all-gather.26.cloned.1.call-start = ((), (), s32[]{:S(2)}) async-start(), calls=%async_computation.18 | async-start | bytes 9437184 | tf_op jit(solution)/shard_map/all_gather | solution.py:99
  318.6 483.2 %copy-start.26 = (f32[256]{0:T(256)}, f32[256]{0:T(256)S(1)}, u32[]{:S(2)}) copy-start(f32[256]{0:T(256)S(1)} %add_rsqrt_fusion) | copy-start | bytes 3076
  320.1 305.8 %all-gather.30.cloned.1.call-start = ((), (), s32[]{:S(2)}) async-start(), calls=%async_computation.20 | async-start | bytes 5242880 | tf_op jit(solution)/shard_map/all_gather | solution.py:117
  322.4 358.7 %all-gather.32.cloned.1.call-start = ((), (), s32[]{:S(2)}) async-start(), calls=%async_computation.22 | async-start | bytes 9437184 | tf_op jit(solution)/shard_map/all_gather | solution.py:99
  383.4 415.7 %reduce-scatter.14.cloned.1.call-start = ((), (), s32[]{:S(2)}) async-start(), calls=%async_computation.23 | async-start | bytes 9437184 | tf_op jit(solution)/shard_map/reduce_scatter | solution.py:103
  727.4 130.8 %all-gather.34.cloned.1.call-start = ((), (), s32[]{:S(2)}) async-start(), calls=%async_computation.24 | async-start | bytes 9437184 | tf_op jit(solution)/shard_map/all_gather | solution.py:99
  803.8 227.6 %reduce-scatter.16.cloned.1.call-start = ((), (), s32[]{:S(2)}) async-start(), calls=%async_computation.25 | async-start | bytes 2621440 | tf_op jit(solution)/shard_map/reduce_scatter | solution.py:121
  980.4 122.1 %reduce-scatter.26.cloned.1.call-start = ((), (), s32[]{:S(2)}) async-start(), calls=%async_computation.34 | async-start | bytes 5242880 | tf_op jit(solution)/shard_map/reduce_scatter | solution.py:121
  994.4 256.1 %reduce-scatter.24.cloned.1.call-start = ((), (), s32[]{:S(2)}) async-start(), calls=%async_computation.31 | async-start | bytes 10485760 | tf_op jit(solution)/shard_map/reduce_scatter | solution.py:121
  1018.4 262.2 %reduce-scatter.22.cloned.1.call-start = ((), (), s32[]{:S(2)}) async-start(), calls=%async_computation.29 | async-start | bytes 1310720 | tf_op jit(solution)/shard_map/reduce_scatter | solution.py:121
  1028.3 326.2 %reduce-scatter.18.cloned.1.call-start = ((), (), s32[]{:S(2)}) async-start(), calls=%async_computation.26 | async-start | bytes 9437184 | tf_op jit(solution)/shard_map/reduce_scatter | solution.py:103
  1040.9 389.0 %reduce-scatter.12.cloned.1.call-start = ((), (), s32[]{:S(2)}) async-start(), calls=%async_computation.21 | async-start | bytes 9437184 | tf_op jit(solution)/shard_map/reduce_scatter | solution.py:103
  1055.2 429.7 %reduce-scatter.20.cloned.1.call-start = ((), (), s32[]{:S(2)}) async-start(), calls=%async_computation.27 | async-start | bytes 1966080 | tf_op jit(solution)/shard_map/reduce_scatter | solution.py:121
  1064.4 478.5 %all-gather.44.cloned.1.call-start = ((), (), s32[]{:S(2)}) async-start(), calls=%async_computation.35 | async-start | bytes 5242880 | tf_op jit(solution)/shard_map/all_gather | solution.py:323
  1102.6 252.0 %copy-start.3 = (f32[4,32,8,512]{3,2,0,1:T(8,128)S(1)}, f32[4,32,8,512]{3,2,0,1:T(8,128)}, u32[]{:S(2)}) copy-start(f32[4,32,8,512]{3,2,0,1:T(8,128)} %copy-done.2) | copy-start | bytes 6291460
  1102.6 251.9 %copy-start.24 = (f32[1,2048]{1,0:T(1,128)S(1)}, f32[1,2048]{1,0:T(1,128)}, u32[]{:S(2)}) copy-start(f32[1,2048]{1,0:T(1,128)} %copy-done.23) | copy-start | bytes 24580
  1102.6 251.9 %copy-start.29 = (f32[256]{0:T(256)S(1)}, f32[256]{0:T(256)}, u32[]{:S(2)}) copy-start(f32[256]{0:T(256)} %copy-done.28) | copy-start | bytes 3076
  1102.6 495.2 %all-gather.40.cloned.1.call-start = ((), (), s32[]{:S(2)}) async-start(), calls=%async_computation.32 | async-start | bytes 5242880 | tf_op jit(solution)/shard_map/all_gather | solution.py:320
  1253.6 399.3 %all-gather.42.cloned.1.call-start = ((), (), s32[]{:S(2)}) async-start(), calls=%async_computation.33 | async-start | bytes 5242880 | tf_op jit(solution)/shard_map/all_gather | solution.py:320
  1254.3 426.9 %all-gather.38.cloned.1.call-start = ((), (), s32[]{:S(2)}) async-start(), calls=%async_computation.30 | async-start | bytes 1310720 | tf_op jit(solution)/shard_map/all_gather | solution.py:323
  1435.5 53.7 %all-to-all-start.1 = ((bf16[256,4,512]{2,0,1:T(8,128)(2,1)}), bf16[256,4,512]{2,0,1:T(8,128)(2,1)S(1)}, u32[]{:S(2)}, u32[]{:S(2)}) async-start(bf16[256,4,512]{2,0,1:T(8,128)(2,1)} %bitcast.185), calls=%async_computation.3 | async-start | bytes 2097152 | tf_op jit(solution)/shard_map/all_to_all | solution.py:113
  1440.1 272.8 %all-gather.36.cloned.1.call-start = ((), (), s32[]{:S(2)}) async-start(), calls=%async_computation.28 | async-start | bytes 1310720 | tf_op jit(solution)/shard_map/all_gather | solution.py:320
  1489.2 266.0 %all-to-all-start.3 = ((bf16[256,4,512]{2,0,1:T(8,128)(2,1)}), bf16[256,4,512]{2,0,1:T(8,128)(2,1)S(1)}, u32[]{:S(2)}, u32[]{:S(2)}) async-start(bf16[256,4,512]{2,0,1:T(8,128)(2,1)} %bitcast.272), calls=%async_computation.8 | async-start | bytes 2097152 | tf_op jit(solution)/shard_map/all_to_all | solution.py:113
  (31 other events, 1088.7 us)
Sparse Core Ops, SparseCore 0:
  16.6 48.6 all-gather.19
  67.8 53.4 all-gather.17
  130.3 46.2 all-gather.21
  178.6 26.1 all-gather.23
  247.2 69.6 reduce-scatter.9
  318.9 169.1 all-gather.27
  490.6 52.3 all-gather.25
  545.1 80.7 all-gather.29
  628.4 52.7 all-gather.31
  727.5 71.4 reduce-scatter.13
  803.9 54.2 all-gather.33
  980.6 43.6 reduce-scatter.15
  1026.5 75.9 reduce-scatter.25
  1105.3 145.1 reduce-scatter.23
  1252.6 27.8 reduce-scatter.21
  1284.4 70.0 reduce-scatter.17
  1358.4 71.4 reduce-scatter.11
  1432.6 52.2 reduce-scatter.19
  1486.8 56.1 all-gather.43
  1545.2 52.5 all-gather.39
  1600.3 52.5 all-gather.41
  1654.7 26.4 all-gather.37
  1683.1 28.7 all-gather.35
